TPU v7x, 128 devices: a whole 4x4x4 slice. The times are simulated.
128 devices in a mesh: row: 8 (over z, x_lo), col: 16 (over x_hi, y, core).
Axes of the slice: x: 4 (x_hi: 2, x_lo: 2; x = x_hi * 2 + x_lo), y: 4, z: 4, core: 2. Of those that a mesh axis runs over, the one named last changes fastest.
Arguments:
- tokens: bfloat16 [8192, 2048], P(('row', 'col')), may hold values from -6 to 6
- timestep: int32 [1], replicated, may hold values from 0 to 999
- mod_weight: float32 [256, 2048], replicated, may hold values from -0.375 to 0.375
- qkv_weight: bfloat16 [3, 2048, 2048], P(None, None, 'col'), may hold values from -0.125 to 0.125
- attn_scale: float32 [16], P('col'), may hold values from 4 to 40
- out_weight: bfloat16 [2048, 2048], P('col'), may hold values from -0.5 to 0.5
- grad_update: bfloat16 [8192, 2048], P(('row', 'col')), may hold values from -6 to 6
Outputs:
- update: bfloat16 [8192, 2048], P(('row', 'col'))
- grad_tokens: bfloat16 [8192, 2048], P(('row', 'col'))
- grad_qkv: float32 [3, 2048, 2048], P(None, 'row', 'col')
- grad_out: float32 [2048, 2048], P('col', 'row')
All inputs are finite; a program needn't handle non-finite values.
Results may differ from a plain program's by a relative error of at most 0.018.
Values may be sent and summed in bfloat16 or wider, within the bound.
No kernel may reach another device: no remote copies, remote signals or barrier semaphores. Data moves between devices by JAX's collectives and lax.ppermute only.
A program may use at most 128 MiB of HBM per device.

v0:
```python
import math
import jax
import jax.numpy as jnp
from jax import lax
from jax.sharding import PartitionSpec as P

epsilon = 1e-06


def sent_together(arrays, axis, dim, along):
    widths = [a.shape[along] for a in arrays]
    both = jnp.concatenate(arrays, axis=along)
    whole = lax.all_gather(both, axis, axis=dim, tiled=True)
    return tuple(jnp.split(whole, [sum(widths[:k]) for k in range(1, len(widths))], axis=along))


def cut_along(shard, dim, count):
    shape = shard.shape
    tiles = shard.reshape(*shape[:dim], count, shape[dim] // count, *shape[dim + 1 :])
    return jnp.moveaxis(tiles, dim, 0)


def sum_at_owner(shard, axis, dim):
    count = lax.axis_size(axis)
    tiles = lax.all_to_all(cut_along(shard, dim, count), axis, 0, 0, tiled=True)
    return jnp.sum(tiles.astype(jnp.float32), axis=0)


def embed(timestep, count):
    index = jnp.arange(count, dtype=jnp.float32)
    freqs = jnp.exp(-math.log(10000.0) * index / count)
    angles = timestep.astype(jnp.float32)[0] * freqs
    return jnp.concatenate([jnp.cos(angles), jnp.sin(angles)])


def unit_rows(values):
    factor = lax.rsqrt(jnp.mean(values * values, -1, keepdims=True) + epsilon)
    return (values * factor, factor)


def unit_grad(grad_unit, unit, factor):
    return factor * (grad_unit - unit * jnp.mean(grad_unit * unit, -1, keepdims=True))


def split_blocks(array, size):
    return array.reshape((array.shape[0] // size, size) + array.shape[1:])


def per_device(tokens, timestep, mod_weight, qkv_weight, attn_scale, out_weight, grad_update):
    tok_dev, width = tokens.shape
    heads_here = attn_scale.shape[0]
    inner = qkv_weight.shape[2]
    head_dim = inner // heads_here
    span = tok_dev * lax.axis_size("col")
    coeff = attn_scale / head_dim
    embedded = embed(timestep, mod_weight.shape[0] // 2)
    gain = 1.0 + jnp.sum(embedded[:, None] * mod_weight, 0)
    tok_float = tokens.astype(jnp.float32)
    rstd = lax.rsqrt(jnp.mean(tok_float * tok_float, -1, keepdims=True) + epsilon)
    normed = tok_float * rstd
    hidden = (normed * gain).astype(jnp.bfloat16)
    group = lax.all_gather(hidden, "col", axis=0, tiled=True)
    raw = jnp.einsum("sd,kdh->ksh", group, qkv_weight, preferred_element_type=jnp.float32)
    query_unit, query_factor = unit_rows(raw[0].reshape(span, heads_here, head_dim))
    key_unit, key_factor = unit_rows(raw[1].reshape(span, heads_here, head_dim))
    queries = query_unit.astype(jnp.bfloat16)
    key_heads = key_unit.astype(jnp.bfloat16)
    value_heads = raw[2].astype(jnp.bfloat16).reshape(span, heads_here, head_dim)
    start_state = (
        jnp.zeros((heads_here, span), jnp.float32),
        jnp.zeros((span, heads_here, head_dim), jnp.float32),
    )
    carry = start_state
    key_piece, value_piece = sent_together((key_heads, value_heads), "row", 0, 1)
    size = math.gcd(key_piece.shape[0], 512)

    def attend_step(state, block):
        key_block, value_block = block
        scores = (
            jnp.einsum("qhd,khd->hqk", queries, key_block, preferred_element_type=jnp.float32)
            * coeff[:, None, None]
        )
        weights = jnp.exp(scores - attn_scale[:, None, None])
        totals = state[0] + jnp.sum(weights, -1)
        mixed = state[1] + jnp.einsum(
            "hqk,khd->qhd",
            weights.astype(jnp.bfloat16),
            value_block,
            preferred_element_type=jnp.float32,
        )
        return ((totals, mixed), None)

    carry, unused = lax.scan(
        attend_step, carry, (split_blocks(key_piece, size), split_blocks(value_piece, size))
    )
    totals, mixed = carry
    attended_heads = (mixed / totals.T[:, :, None]).astype(jnp.bfloat16)
    attended = attended_heads.reshape(span, inner)
    own_rows = lax.all_to_all(attended, "col", split_axis=0, concat_axis=1, tiled=True)
    update = jnp.dot(
        own_rows,
        lax.all_gather(out_weight, "col", axis=0, tiled=True),
        preferred_element_type=jnp.float32,
    ).astype(jnp.bfloat16)
    grad_group = lax.all_gather(grad_update, "col", axis=0, tiled=True)
    out_part = lax.dot_general(
        attended, grad_group, (((0,), (0,)), ((), ())), preferred_element_type=jnp.float32
    )
    grad_out = sum_at_owner(out_part.astype(jnp.bfloat16), "row", 1)
    grad_attended = lax.dot_general(
        grad_group, out_weight, (((1,), (1,)), ((), ())), preferred_element_type=jnp.float32
    ).astype(jnp.bfloat16)
    grad_heads = grad_attended.reshape(span, heads_here, head_dim)
    delta = jnp.sum(grad_heads.astype(jnp.float32) * attended_heads.astype(jnp.float32), -1)
    inverse = 1.0 / totals

    def pair_terms(query_rows, grad_rows, inverse_rows, delta_rows, key_block, value_block):
        scores = (
            jnp.einsum("qhd,khd->hqk", query_rows, key_block, preferred_element_type=jnp.float32)
            * coeff[:, None, None]
        )
        probs = jnp.exp(scores - attn_scale[:, None, None]) * inverse_rows[:, :, None]
        dprobs = jnp.einsum(
            "qhd,khd->hqk", grad_rows, value_block, preferred_element_type=jnp.float32
        )
        dscores = (probs * (dprobs - delta_rows[:, :, None]) * coeff[:, None, None]).astype(
            jnp.bfloat16
        )
        return (probs, dscores)

    empty_own = jnp.zeros((span, heads_here, head_dim), jnp.float32)
    carry = empty_own
    key_piece, value_piece = sent_together((key_heads, value_heads), "row", 0, 1)
    size = math.gcd(key_piece.shape[0], 512)

    def query_step(state, block):
        key_block, value_block = block
        probs, dscores = pair_terms(queries, grad_heads, inverse, delta.T, key_block, value_block)
        return (
            state
            + jnp.einsum("hqk,khd->qhd", dscores, key_block, preferred_element_type=jnp.float32),
            None,
        )

    carry, unused = lax.scan(
        query_step, carry, (split_blocks(key_piece, size), split_blocks(value_piece, size))
    )
    grad_query = carry
    all_inverse, all_delta = sent_together((inverse.T, delta), "row", 0, 1)
    carry = (empty_own, empty_own)
    query_piece, grad_piece = sent_together((queries, grad_heads), "row", 0, 1)
    count = query_piece.shape[0]
    size = math.gcd(count, 512)

    def key_step(state, block):
        query_block, grad_block, inverse_block, delta_block = block
        probs, dscores = pair_terms(
            query_block, grad_block, inverse_block.T, delta_block.T, key_heads, value_heads
        )
        grad_key = state[0] + jnp.einsum(
            "hqk,qhd->khd", dscores, query_block, preferred_element_type=jnp.float32
        )
        grad_value = state[1] + jnp.einsum(
            "hqk,qhd->khd",
            probs.astype(jnp.bfloat16),
            grad_block,
            preferred_element_type=jnp.float32,
        )
        return ((grad_key, grad_value), None)

    carry, unused = lax.scan(
        key_step,
        carry,
        (
            split_blocks(query_piece, size),
            split_blocks(grad_piece, size),
            split_blocks(all_inverse, size),
            split_blocks(all_delta, size),
        ),
    )
    grad_key, grad_value = carry
    grad_q = (
        unit_grad(grad_query, query_unit, query_factor).astype(jnp.bfloat16).reshape(span, inner)
    )
    grad_k = unit_grad(grad_key, key_unit, key_factor).astype(jnp.bfloat16).reshape(span, inner)
    grad_v = grad_value.astype(jnp.bfloat16).reshape(span, inner)
    grad_raw = jnp.stack([grad_q, grad_k, grad_v])
    qkv_part = jnp.einsum("sd,ksh->kdh", group, grad_raw, preferred_element_type=jnp.float32)
    grad_qkv = sum_at_owner(qkv_part.astype(jnp.bfloat16), "row", 1)
    grad_hidden = lax.psum_scatter(
        jnp.einsum("ksh,kdh->sd", grad_raw, qkv_weight, preferred_element_type=jnp.float32).astype(
            jnp.bfloat16
        ),
        "col",
        scatter_dimension=0,
        tiled=True,
    ).astype(jnp.float32)
    grad_normed = grad_hidden * gain
    grad_tokens = (
        rstd * (grad_normed - normed * jnp.mean(grad_normed * normed, -1, keepdims=True))
    ).astype(jnp.bfloat16)
    return (update, grad_tokens, grad_qkv, grad_out)


def solution(mesh):
    placed = (
        P(("row", "col"), None),
        P(),
        P(),
        P(None, None, "col"),
        P("col"),
        P("col", None),
        P(("row", "col"), None),
    )
    return jax.shard_map(
        per_device,
        mesh=mesh,
        in_specs=placed,
        out_specs=(
            P(("row", "col"), None),
            P(("row", "col"), None),
            P(None, "row", "col"),
            P("col", "row"),
        ),
        check_vma=False,
    )
```

profile of v0, /device:TPU:0, one launch (start us, length us, event | category | flops | bytes accessed | tf_op | source)
XLA Modules:
  0.0 560.1 jit_solution(7226077583093130001)
XLA Ops:
  11.7 56.6 %all-gather.6.cloned.1.call-done = bf16[1024,2048]{1,0:T(8,128)(2,1)} async-done(((bf16[64,2048]{1,0:T(8,128)(2,1)}), bf16[1024,2048]{1,0:T(8,128)(2,1)}) %all-gather.6.cloned.1.call-update) | async-done | bytes 4194320 | tf_op jit(solution)/shard_map/all_gather | solution.py:62
  68.3 4.0 fusion.93
  76.1 87.4 %all-gather.8.cloned.1.call-done = bf16[8192,2,128]{0,2,1:T(8,128)(2,1)} async-done(((bf16[1024,2,128]{0,2,1:T(8,128)(2,1)}), bf16[8192,2,128]{0,2,1:T(8,128)(2,1)}) %all-gather.8.cloned.1.call-update) | async-done | bytes 4194320 | tf_op jit(solution)/shard_map/all_gather | solution.py:13
  163.5 3.9 fusion.91
  167.4 4.1 copy.61
  171.5 2.5 copy.62
  174.0 68.0 %while.37 = (s32[]{:T(128)}, f32[1,1024]{1,0:T(1,128)S(1)}, f32[1024,1,128]{0,2,1:T(8,128)S(1)}, bf16[16,512,1,128]{3,1,2,0:T(8,128)(2,1)}, bf16[1024,1,128]{2,0...) while((s32[]{:T(128)}, f32[1,1024]{1,0:T(1,128)S(1)}, ...), condition=%wide.region_6.7_spmd.clone, body=%wide.region_4.6_spmd.clone.sunk | while | flops 271844352 | bytes 5786736 | solution.py:93
  174.0 2.1 fusion.126
  176.1 2.1 fusion.128
  178.2 2.1 fusion.126
  180.3 2.1 fusion.128
  182.5 2.1 fusion.126
  184.6 2.1 fusion.128
  188.8 2.1 fusion.128
  191.0 2.1 fusion.126
  193.1 2.1 fusion.128
  197.3 2.1 fusion.128
  201.6 2.1 fusion.128
  205.8 2.1 fusion.128
  208.0 2.1 fusion.126
  210.0 2.1 fusion.128
  212.2 2.1 fusion.126
  214.3 2.1 fusion.128
  218.6 2.1 fusion.128
  222.8 2.1 fusion.128
  227.1 2.1 fusion.128
  231.3 2.1 fusion.128
  235.6 2.1 fusion.128
  239.8 2.1 fusion.128
  242.0 4.5 multiply_reduce_fusion.3
  250.6 79.5 %while.38 = (s32[]{:T(128)}, f32[1024,1,128]{0,2,1:T(8,128)}, bf16[16,512,1,128]{3,1,2,0:T(8,128)(2,1)}, bf16[1024,1,128]{2,0,1:T(8,128)(2,1)S(1)}, f32[1]{0:T(1...) while((s32[]{:T(128)}, f32[1024,1,128]{0,2,1:T(8,128)}, ...), condition=%wide.region_9.10_spmd.clone, body=%wide.region_8.9_spmd.clone.sunk | while | flops 406585344 | bytes 6171263 | solution.py:145
  251.9 3.5 fusion.135
  256.7 3.6 fusion.135
  261.7 3.7 fusion.135
  266.7 3.6 fusion.135
  271.7 3.6 fusion.135
  276.6 3.6 fusion.135
  281.6 3.6 fusion.135
  286.6 3.6 fusion.135
  291.6 3.6 fusion.135
  296.5 3.6 fusion.135
  301.5 3.6 fusion.135
  306.5 3.7 fusion.135
  311.5 3.6 fusion.135
  316.5 3.6 fusion.135
  321.4 3.6 fusion.135
  326.4 3.6 fusion.135
  330.1 28.7 %all_gather.24 = f32[8192,2]{0,1:T(2,128)S(1)} all-gather(f32[1024,2]{0,1:T(2,128)S(1)} %pad_maximum_fusion.5), channel_id=1, replica_groups=mesh['row'=8,'col'=16] {'row'}, dimensions={0}, use_global_device_ids=true | all-gather | bytes 73728 | tf_op jit(solution)/shard_map/all_gather | solution.py:13
  358.9 3.9 fusion.90
  362.8 4.1 copy.59
  366.9 2.4 copy.60
  369.3 82.8 %while.39 = (s32[]{:T(128)}, f32[1024,1,128]{0,2,1:T(8,128)S(1)}, f32[1024,1,128]{0,2,1:T(8,128)S(1)}, bf16[16,512,1,128]{3,1,2,0:T(8,128)(2,1)}, bf16[1024,1,12...) while((s32[]{:T(128)}, f32[1024,1,128]{0,2,1:T(8,128)S(1)}, ...), condition=%wide.region_12.13_spmd.clone, body=%wide.region_11.12_spmd.clone.sunk | while | flops 541589504 | bytes 9453196 | solution.py:171
  390.0 2.1 exponential_multiply_fusion.3
  455.3 4.3 bitcast_convert_fusion
  461.4 6.6 %all-to-all-start = ((bf16[16,64,128]{2,1,0:T(8,128)(2,1)}), bf16[16,64,128]{2,1,0:T(8,128)(2,1)S(1)}, u32[]{:S(2)}, u32[]{:S(2)}) async-start(bf16[16,64,128]{2,1,0:T(8,128)(2,1)} %bitcast.10), calls=%async_computation | async-start | bytes 524288 | tf_op jit(solution)/shard_map/all_to_all | solution.py:99
  468.0 3.1 convolution_convert_fusion
  472.0 5.5 all-to-all-done
  477.5 3.5 all-to-all-start.2
  481.0 4.1 fusion.63
  486.4 4.6 all-to-all-done.2
  491.1 3.6 all-to-all-start.1
  495.4 5.7 %convolution_convert_fusion.1 = bf16[64,2048]{1,0:T(8,128)(2,1)} fusion(bf16[2048,2048]{1,0:T(8,128)(2,1)} %all-gather.10.cloned.1.call-done, bf16[16,64,128]{2,1,0:T(8,128)(2,1)S(1)} %all-to-all-done), kind=kOutput, calls=%fused_computation.67 | convolution fusion | flops 537001984 | bytes 8912896 | tf_op jit(solution)/shard_map/dot_general | solution.py:100
  501.1 24.3 %all-to-all-done.1 = bf16[8,3,256,128]{2,3,1,0:T(8,128)(2,1)S(1)} async-done(((bf16[8,3,256,128]{2,3,1,0:T(8,128)(2,1)}), bf16[8,3,256,128]{2,3,1,0:T(8,128)(2,1)S(1)}, u32[]{:S(2)}, u32[]{:S(2)}) %all-to-all-start.1) | async-done | bytes 1572896 | tf_op jit(solution)/shard_map/all_to_all | solution.py:25
  526.5 23.7 %reduce-scatter.2.cloned.1.call-done = bf16[64,2048]{1,0:T(8,128)(2,1)} async-done(((bf16[1024,2048]{1,0:T(8,128)(2,1)}), bf16[64,2048]{1,0:T(8,128)(2,1)}) %reduce-scatter.2.cloned.1.call-update) | async-done | bytes 262160 | tf_op jit(solution)/shard_map/reduce_scatter | solution.py:190
  (184 shorter events, 145.2 us)
Async XLA Ops:
  7.2 2.7 copy-start.3
  7.2 3.8 copy-start.8
  7.2 61.1 %all-gather.6.cloned.1.call-start = ((), (), s32[]{:S(2)}) async-start(), calls=%async_computation.4 | async-start | bytes 4456448 | tf_op jit(solution)/shard_map/all_gather | solution.py:62
  10.9 152.6 %all-gather.8.cloned.1.call-start = ((), (), s32[]{:S(2)}) async-start(), calls=%async_computation.5 | async-start | bytes 4718592 | tf_op jit(solution)/shard_map/all_gather | solution.py:13
  72.3 1.2 copy-start
  73.6 2.5 copy-start.5
  74.5 167.5 %all-gather.12.cloned.1.call-start = ((), (), s32[]{:S(2)}) async-start(), calls=%async_computation.7 | async-start | bytes 4456448 | tf_op jit(solution)/shard_map/all_gather | solution.py:105
  75.2 283.6 %all-gather.14.cloned.1.call-start = ((), (), s32[]{:S(2)}) async-start(), calls=%async_computation.8 | async-start | bytes 4718592 | tf_op jit(solution)/shard_map/all_gather | solution.py:13
  242.0 4.5 copy-start.6
  247.3 248.1 %all-gather.10.cloned.1.call-start = ((), (), s32[]{:S(2)}) async-start(), calls=%async_computation.6 | async-start | bytes 8912896 | tf_op jit(solution)/shard_map/all_gather | solution.py:102
  247.9 302.3 %reduce-scatter.2.cloned.1.call-start = ((), (), s32[]{:S(2)}) async-start(), calls=%async_computation.9 | async-start | bytes 4456448 | tf_op jit(solution)/shard_map/reduce_scatter | solution.py:190
  366.9 2.4 copy-start.2
  452.1 1.9 copy-start.1
  452.1 2.0 copy-start.7
  453.8 1.5 copy-start.9
  459.6 0.9 copy-start.10
  461.4 16.1 %all-to-all-start = ((bf16[16,64,128]{2,1,0:T(8,128)(2,1)}), bf16[16,64,128]{2,1,0:T(8,128)(2,1)S(1)}, u32[]{:S(2)}, u32[]{:S(2)}) async-start(bf16[16,64,128]{2,1,0:T(8,128)(2,1)} %bitcast.10), calls=%async_computation | async-start | bytes 524288 | tf_op jit(solution)/shard_map/all_to_all | solution.py:99
  477.5 13.6 %all-to-all-start.2 = ((bf16[8,128,256]{2,1,0:T(8,128)(2,1)}), bf16[8,128,256]{2,1,0:T(8,128)(2,1)S(1)}, u32[]{:S(2)}, u32[]{:S(2)}) async-start(bf16[8,128,256]{2,1,0:T(8,128)(2,1)} %bitcast.177), calls=%async_computation.3 | async-start | bytes 1048576 | tf_op jit(solution)/shard_map/all_to_all | solution.py:25
  491.1 34.3 %all-to-all-start.1 = ((bf16[8,3,256,128]{2,3,1,0:T(8,128)(2,1)}), bf16[8,3,256,128]{2,3,1,0:T(8,128)(2,1)S(1)}, u32[]{:S(2)}, u32[]{:S(2)}) async-start(bf16[8,3,256,128]{2,3,1,0:T(8,128)(2,1)} %bitcast.175), calls=%async_computation.2 | async-start | bytes 3145728 | tf_op jit(solution)/shard_map/all_to_all | solution.py:25
  501.1 49.1 %copy-start.4 = (bf16[64,2048]{1,0:T(8,128)(2,1)S(1)}, bf16[64,2048]{1,0:T(8,128)(2,1)}, u32[]{:S(2)}) copy-start(bf16[64,2048]{1,0:T(8,128)(2,1)} %param.13) | copy-start | bytes 786436
Sparse Core Ops, SparseCore 0:
  11.1 57.1 all-gather.5
  74.6 88.8 all-gather.7
  166.0 54.3 all-gather.11
  247.5 90.8 all-gather.13
  340.7 72.3 all-gather.9
  459.8 90.3 reduce-scatter.1
where the time goes:
time: 564 us; the launch traced here: 560 us
  matrix products  254 us (45%)
  waiting for transfers between devices  203 us (36%)
  local copies, waits for them, and re-layouts  31.6 us (6%)
  blocking collectives  28.7 us (5%)
  between operations  15.9 us (3%)
  starting transfers between devices  13.9 us (2%)
  other arithmetic  11 us (2%)
    all_gather x2, waiting for transfers between devices, sent_together(): whole = lax.all_gather(both, axis, axis=dim, tiled=True)  87.4 us
    dot_general x16, matrix products, query_step(): jnp.einsum('hqk,khd->qhd', dscores, key_block, preferred_element_type=jnp...  57.9 us
    all_gather x1, waiting for transfers between devices, per_device(): group = lax.all_gather(hidden, 'col', axis=0, tiled=True)  56.6 us
    dot_general x32, matrix products, pair_terms(): jnp.einsum('qhd,khd->hqk', query_rows, key_block, preferred_element_type=...  54.5 us
    dot_general x16, matrix products, attend_step(): jnp.einsum('hqk,khd->qhd', weights.astype(jnp.bfloat16), value_block, pre...  33.9 us
    dot_general x16, matrix products, attend_step(): jnp.einsum('qhd,khd->hqk', queries, key_block, preferred_element_type=jnp...  33.2 us
    all_to_all x2, waiting for transfers between devices, sum_at_owner(): tiles = lax.all_to_all(cut_along(shard, dim, count), axis, 0, 0, tiled=True)  28.9 us
    all_gather x1, blocking collectives, sent_together(): whole = lax.all_gather(both, axis, axis=dim, tiled=True)  28.7 us
  transfers between devices with their start and end apart: 9, of which 6 were waited for; matrix products, arithmetic and copies ran while one was open for 49% of the time, Pallas kernels for 0%

commit v1 on v0

--- a/solution.py
+++ b/solution.py
@@ -59,7 +59,9 @@
     rstd = lax.rsqrt(jnp.mean(tok_float * tok_float, -1, keepdims=True) + epsilon)
     normed = tok_float * rstd
     hidden = (normed * gain).astype(jnp.bfloat16)
-    group = lax.all_gather(hidden, "col", axis=0, tiled=True)
+    group = jnp.concatenate(
+        lax.all_to_all(jnp.stack([hidden] * lax.axis_size("col")), "col", 0, 0), axis=0
+    )
     raw = jnp.einsum("sd,kdh->ksh", group, qkv_weight, preferred_element_type=jnp.float32)
     query_unit, query_factor = unit_rows(raw[0].reshape(span, heads_here, head_dim))
     key_unit, key_factor = unit_rows(raw[1].reshape(span, heads_here, head_dim))

time: 564 us -> 581 us (1.030)
  waiting for transfers between devices: 203 us -> 212 us
  starting transfers between devices: 13.9 us -> 21.3 us
    all_gather x1 -> x0, waiting for transfers between devices: 56.6 us -> none  [per_device(): group = lax.all_gather(hidden, 'col', axis=0, tiled=True)]
    all_to_all x0 -> x1, waiting for transfers between devices: none -> 55.1 us  [per_device(): lax.all_to_all(jnp.stack([hidden] * lax.axis_size('col')), 'col', 0, 0)]
    all_gather x2, waiting for transfers between devices: 87.4 us -> 97.4 us  [sent_together(): whole = lax.all_gather(both, axis, axis=dim, tiled=True)]
    all_to_all x0 -> x1, starting transfers between devices: none -> 7.33 us  [per_device(): lax.all_to_all(jnp.stack([hidden] * lax.axis_size('col')), 'col', 0, 0)]
  transfers between devices with their start and end apart: 9 -> 9, of which waited for: 6 -> 6; matrix products, arithmetic and copies ran while one was open for 49% -> 48% of each run, Pallas kernels for 0% -> 0%
where the time goes in v1:
time: 581 us; the launch traced here: 577 us
  matrix products  254 us (44%)
  waiting for transfers between devices  212 us (36%)
  local copies, waits for them, and re-layouts  34.1 us (6%)
  blocking collectives  28.7 us (5%)
  starting transfers between devices  21.3 us (4%)
  between operations  15.5 us (3%)
  other arithmetic  10.3 us (2%)
    all_gather x2, waiting for transfers between devices, sent_together(): whole = lax.all_gather(both, axis, axis=dim, tiled=True)  97.4 us
    dot_general x16, matrix products, query_step(): jnp.einsum('hqk,khd->qhd', dscores, key_block, preferred_element_type=jnp...  58 us
    all_to_all x1, waiting for transfers between devices, per_device(): lax.all_to_all(jnp.stack([hidden] * lax.axis_size('col')), 'col', 0, 0)  55.1 us
    dot_general x32, matrix products, pair_terms(): jnp.einsum('qhd,khd->hqk', query_rows, key_block, preferred_element_type=...  54.5 us
    dot_general x16, matrix products, attend_step(): jnp.einsum('hqk,khd->qhd', weights.astype(jnp.bfloat16), value_block, pre...  33.9 us
    dot_general x16, matrix products, attend_step(): jnp.einsum('qhd,khd->hqk', queries, key_block, preferred_element_type=jnp...  33.2 us
    all_to_all x2, waiting for transfers between devices, sum_at_owner(): tiles = lax.all_to_all(cut_along(shard, dim, count), axis, 0, 0, tiled=True)  28.9 us
    all_gather x1, blocking collectives, sent_together(): whole = lax.all_gather(both, axis, axis=dim, tiled=True)  28.7 us
  transfers between devices with their start and end apart: 9, of which 6 were waited for; matrix products, arithmetic and copies ran while one was open for 48% of the time, Pallas kernels for 0%

profile of v1, /device:TPU:0, one launch (start us, length us, event | category | flops | bytes accessed | tf_op | source)
XLA Modules:
  0.0 577.3 jit_solution(15221502240902268478)
XLA Ops:
  10.1 2.5 stack.4
  12.6 7.3 %all-to-all-start = ((bf16[16,64,2048]{2,1,0:T(8,128)(2,1)}), bf16[16,64,2048]{2,1,0:T(8,128)(2,1)}, u32[]{:S(2)}, u32[]{:S(2)}) async-start(bf16[16,64,2048]{2,1,0:T(8,128)(2,1)} %stack.4), calls=%async_computation | async-start | bytes 8388608 | tf_op jit(solution)/shard_map/all_to_all | solution.py:63
  20.7 55.1 %all-to-all-done = bf16[16,64,2048]{2,1,0:T(8,128)(2,1)} async-done(((bf16[16,64,2048]{2,1,0:T(8,128)(2,1)}), bf16[16,64,2048]{2,1,0:T(8,128)(2,1)}, u32[]{:S(2)}, u32[]{:S(2)}) %all-to-all-start) | async-done | bytes 4194336 | tf_op jit(solution)/shard_map/all_to_all | solution.py:63
  75.8 4.0 fusion.88
  83.6 97.3 %all-gather.5.cloned.1.call-done = bf16[8192,2,128]{0,2,1:T(8,128)(2,1)} async-done(((bf16[1024,2,128]{0,2,1:T(8,128)(2,1)}), bf16[8192,2,128]{0,2,1:T(8,128)(2,1)}) %all-gather.5.cloned.1.call-update) | async-done | bytes 4194320 | tf_op jit(solution)/shard_map/all_gather | solution.py:13
  181.0 3.9 fusion.86
  184.9 4.1 copy.61
  188.9 2.5 copy.62
  191.4 68.0 %while.37 = (s32[]{:T(128)}, f32[1,1024]{1,0:T(1,128)S(1)}, f32[1024,1,128]{0,2,1:T(8,128)S(1)}, bf16[16,512,1,128]{3,1,2,0:T(8,128)(2,1)}, bf16[1024,1,128]{2,0...) while((s32[]{:T(128)}, f32[1,1024]{1,0:T(1,128)S(1)}, ...), condition=%wide.region_6.7_spmd.clone, body=%wide.region_4.6_spmd.clone.sunk | while | flops 271844352 | bytes 5786736 | solution.py:95
  191.4 2.1 fusion.122
  193.5 2.1 fusion.124
  195.7 2.1 fusion.122
  197.8 2.1 fusion.124
  202.0 2.1 fusion.124
  206.3 2.1 fusion.124
  210.5 2.1 fusion.124
  214.8 2.1 fusion.124
  219.0 2.1 fusion.124
  223.3 2.1 fusion.124
  225.4 2.1 fusion.122
  227.5 2.1 fusion.124
  229.7 2.1 fusion.122
  231.8 2.1 fusion.124
  236.0 2.1 fusion.124
  240.3 2.1 fusion.124
  244.5 2.1 fusion.124
  248.8 2.1 fusion.124
  253.0 2.1 fusion.124
  257.3 2.1 fusion.124
  259.4 4.5 multiply_reduce_fusion.3
  268.0 79.5 %while.38 = (s32[]{:T(128)}, f32[1024,1,128]{0,2,1:T(8,128)}, bf16[16,512,1,128]{3,1,2,0:T(8,128)(2,1)}, bf16[1024,1,128]{2,0,1:T(8,128)(2,1)S(1)}, f32[1]{0:T(1...) while((s32[]{:T(128)}, f32[1024,1,128]{0,2,1:T(8,128)}, ...), condition=%wide.region_9.10_spmd.clone, body=%wide.region_8.9_spmd.clone.sunk | while | flops 406585344 | bytes 6171263 | solution.py:147
  269.4 3.5 fusion.131
  274.2 3.6 fusion.131
  279.2 3.7 fusion.131
  284.2 3.6 fusion.131
  289.1 3.6 fusion.131
  294.1 3.6 fusion.131
  299.1 3.6 fusion.131
  304.1 3.6 fusion.131
  309.1 3.6 fusion.131
  314.0 3.6 fusion.131
  319.0 3.6 fusion.131
  324.0 3.7 fusion.131
  329.0 3.6 fusion.131
  333.9 3.6 fusion.131
  338.9 3.6 fusion.131
  343.9 3.6 fusion.131
  347.5 28.7 %all_gather.20 = f32[8192,2]{0,1:T(2,128)S(1)} all-gather(f32[1024,2]{0,1:T(2,128)S(1)} %pad_maximum_fusion.5), channel_id=1, replica_groups=mesh['row'=8,'col'=16] {'row'}, dimensions={0}, use_global_device_ids=true | all-gather | bytes 73728 | tf_op jit(solution)/shard_map/all_gather | solution.py:13
  376.3 3.9 fusion.85
  380.3 4.1 copy.59
  384.3 2.4 copy.60
  386.8 82.8 %while.39 = (s32[]{:T(128)}, f32[1024,1,128]{0,2,1:T(8,128)S(1)}, f32[1024,1,128]{0,2,1:T(8,128)S(1)}, bf16[16,512,1,128]{3,1,2,0:T(8,128)(2,1)}, bf16[1024,1,12...) while((s32[]{:T(128)}, f32[1024,1,128]{0,2,1:T(8,128)S(1)}, ...), condition=%wide.region_12.13_spmd.clone, body=%wide.region_11.12_spmd.clone.sunk | while | flops 541589504 | bytes 9453196 | solution.py:173
  407.5 2.1 exponential_multiply_fusion.3
  472.8 4.3 bitcast_convert_fusion
  478.9 6.6 %all-to-all-start.1 = ((bf16[16,64,128]{2,1,0:T(8,128)(2,1)}), bf16[16,64,128]{2,1,0:T(8,128)(2,1)S(1)}, u32[]{:S(2)}, u32[]{:S(2)}) async-start(bf16[16,64,128]{2,1,0:T(8,128)(2,1)} %bitcast.11), calls=%async_computation.1 | async-start | bytes 524288 | tf_op jit(solution)/shard_map/all_to_all | solution.py:101
  485.5 3.1 convolution_convert_fusion.1
  489.5 5.5 all-to-all-done.1
  495.0 3.5 all-to-all-start.3
  498.5 4.1 convolution_convert_fusion
  503.9 4.6 all-to-all-done.3
  508.6 3.6 all-to-all-start.2
  512.9 5.7 convolution_convert_fusion.2
  518.6 24.3 %all-to-all-done.2 = bf16[8,3,256,128]{2,3,1,0:T(8,128)(2,1)S(1)} async-done(((bf16[8,3,256,128]{2,3,1,0:T(8,128)(2,1)}), bf16[8,3,256,128]{2,3,1,0:T(8,128)(2,1)S(1)}, u32[]{:S(2)}, u32[]{:S(2)}) %all-to-all-start.2) | async-done | bytes 1572896 | tf_op jit(solution)/shard_map/all_to_all | solution.py:25
  544.0 23.8 %reduce-scatter.2.cloned.1.call-done = bf16[64,2048]{1,0:T(8,128)(2,1)} async-done(((bf16[1024,2048]{1,0:T(8,128)(2,1)}), bf16[64,2048]{1,0:T(8,128)(2,1)}) %reduce-scatter.2.cloned.1.call-update) | async-done | bytes 262160 | tf_op jit(solution)/shard_map/reduce_scatter | solution.py:192
  (184 shorter events, 148.6 us)
Async XLA Ops:
  7.2 2.6 copy-start.3
  12.6 7.4 %copy-start.8 = (bf16[3,2048,128]{2,1,0:T(8,128)(2,1)S(1)}, bf16[3,2048,128]{2,1,0:T(8,128)(2,1)}, u32[]{:S(2)}) copy-start(bf16[3,2048,128]{2,1,0:T(8,128)(2,1)} %param.16) | copy-start | bytes 4718596
  12.6 63.2 %all-to-all-start = ((bf16[16,64,2048]{2,1,0:T(8,128)(2,1)}), bf16[16,64,2048]{2,1,0:T(8,128)(2,1)}, u32[]{:S(2)}, u32[]{:S(2)}) async-start(bf16[16,64,2048]{2,1,0:T(8,128)(2,1)} %stack.4), calls=%async_computation | async-start | bytes 8388608 | tf_op jit(solution)/shard_map/all_to_all | solution.py:63
  19.9 161.1 %all-gather.5.cloned.1.call-start = ((), (), s32[]{:S(2)}) async-start(), calls=%async_computation.5 | async-start | bytes 4718592 | tf_op jit(solution)/shard_map/all_gather | solution.py:13
  79.8 1.2 copy-start
  81.1 2.6 copy-start.5
  82.0 177.5 %all-gather.9.cloned.1.call-start = ((), (), s32[]{:S(2)}) async-start(), calls=%async_computation.7 | async-start | bytes 4456448 | tf_op jit(solution)/shard_map/all_gather | solution.py:107
  82.7 293.6 %all-gather.11.cloned.1.call-start = ((), (), s32[]{:S(2)}) async-start(), calls=%async_computation.8 | async-start | bytes 4718592 | tf_op jit(solution)/shard_map/all_gather | solution.py:13
  259.4 4.5 copy-start.6
  264.8 248.1 %all-gather.7.cloned.1.call-start = ((), (), s32[]{:S(2)}) async-start(), calls=%async_computation.6 | async-start | bytes 8912896 | tf_op jit(solution)/shard_map/all_gather | solution.py:104
  265.4 302.3 %reduce-scatter.2.cloned.1.call-start = ((), (), s32[]{:S(2)}) async-start(), calls=%async_computation.9 | async-start | bytes 4456448 | tf_op jit(solution)/shard_map/reduce_scatter | solution.py:192
  384.3 2.4 copy-start.2
  469.5 1.9 copy-start.1
  469.6 2.0 copy-start.7
  471.3 1.5 copy-start.9
  477.1 0.9 copy-start.10
  478.9 16.1 %all-to-all-start.1 = ((bf16[16,64,128]{2,1,0:T(8,128)(2,1)}), bf16[16,64,128]{2,1,0:T(8,128)(2,1)S(1)}, u32[]{:S(2)}, u32[]{:S(2)}) async-start(bf16[16,64,128]{2,1,0:T(8,128)(2,1)} %bitcast.11), calls=%async_computation.1 | async-start | bytes 524288 | tf_op jit(solution)/shard_map/all_to_all | solution.py:101
  495.0 13.6 %all-to-all-start.3 = ((bf16[8,128,256]{2,1,0:T(8,128)(2,1)}), bf16[8,128,256]{2,1,0:T(8,128)(2,1)S(1)}, u32[]{:S(2)}, u32[]{:S(2)}) async-start(bf16[8,128,256]{2,1,0:T(8,128)(2,1)} %bitcast.176), calls=%async_computation.4 | async-start | bytes 1048576 | tf_op jit(solution)/shard_map/all_to_all | solution.py:25
  508.6 34.3 %all-to-all-start.2 = ((bf16[8,3,256,128]{2,3,1,0:T(8,128)(2,1)}), bf16[8,3,256,128]{2,3,1,0:T(8,128)(2,1)S(1)}, u32[]{:S(2)}, u32[]{:S(2)}) async-start(bf16[8,3,256,128]{2,3,1,0:T(8,128)(2,1)} %bitcast.174), calls=%async_computation.3 | async-start | bytes 3145728 | tf_op jit(solution)/shard_map/all_to_all | solution.py:25
  518.6 49.1 %copy-start.4 = (bf16[64,2048]{1,0:T(8,128)(2,1)S(1)}, bf16[64,2048]{1,0:T(8,128)(2,1)}, u32[]{:S(2)}) copy-start(bf16[64,2048]{1,0:T(8,128)(2,1)} %param.13) | copy-start | bytes 786436
Sparse Core Ops, SparseCore 0:
  82.1 98.8 all-gather.4
  183.4 54.3 all-gather.8
  264.9 90.8 all-gather.10
  358.2 72.3 all-gather.6
  477.2 90.4 reduce-scatter.1
